TPU v7x, 32 devices: a whole 2x2x4 slice. The times are simulated.
32 devices in a mesh: dp: 8 (over z, x), seq: 4 (over y, core).
Axes of the slice: x: 2, y: 2, z: 4, core: 2. Of those that a mesh axis runs over, the one named last changes fastest.
Arguments:
- tokens: bfloat16 [16384, 1024], P(('dp', 'seq')), may hold values from -6 to 6
- time_embed: bfloat16 [32, 1024], P(('dp', 'seq')), may hold values from -6 to 6
- lengths: int32 [32], P('dp'), may hold values from 0 to 475, as said below
- cotangent: bfloat16 [16384, 1024], P(('dp', 'seq')), may hold values from -6 to 6
- w_query: bfloat16 [1024, 1024], P('seq'), may hold values from -0.1875 to 0.1875
- w_key: bfloat16 [1024, 1024], P('seq'), may hold values from -0.1875 to 0.1875
- w_value: bfloat16 [1024, 1024], P('seq'), may hold values from -0.1875 to 0.1875
- w_out: bfloat16 [1024, 1024], P('seq'), may hold values from -0.75 to 0.75
- w_time: bfloat16 [1024, 1024], P('seq'), may hold values from -0.1875 to 0.1875
- w_in: bfloat16 [4096, 1024], P('seq'), may hold values from -0.1875 to 0.1875
- w_down: bfloat16 [4096, 1024], P('seq'), may hold values from -0.09375 to 0.09375
- b_query: bfloat16 [1024], replicated, may hold values from -3 to 3
- b_value: bfloat16 [1024], replicated, may hold values from -3 to 3
- b_out: bfloat16 [1024], replicated, may hold values from -3 to 3
- b_time: bfloat16 [1024], replicated, may hold values from -3 to 3
- b_in: bfloat16 [4096], replicated, may hold values from -3 to 3
- b_down: bfloat16 [1024], replicated, may hold values from -2 to 2
- gain_one: bfloat16 [1024], replicated, may hold values from 0.25 to 1.75
- shift_one: bfloat16 [1024], replicated, may hold values from -2 to 2
- gain_two: bfloat16 [1024], replicated, may hold values from 0.25 to 1.75
- shift_two: bfloat16 [1024], replicated, may hold values from -2 to 2
Outputs:
- layer_out: bfloat16 [16384, 1024], P(('dp', 'seq'))
- grad_tokens: bfloat16 [16384, 1024], P(('dp', 'seq'))
- grad_w_query: float32 [1024, 1024], P('seq')
- grad_w_key: float32 [1024, 1024], P('seq')
- grad_w_value: float32 [1024, 1024], P('seq')
- grad_w_out: float32 [1024, 1024], P('seq')
- grad_w_time: float32 [1024, 1024], P('seq')
- grad_w_in: float32 [4096, 1024], P('seq')
- grad_w_down: float32 [4096, 1024], P('seq')
- grad_b_query: float32 [1024], replicated
- grad_b_value: float32 [1024], replicated
- grad_b_out: float32 [1024], replicated
- grad_b_time: float32 [1024], replicated
- grad_b_in: float32 [4096], replicated
- grad_b_down: float32 [1024], replicated
- grad_gain_one: float32 [1024], replicated
- grad_shift_one: float32 [1024], replicated
- grad_gain_two: float32 [1024], replicated
- grad_shift_two: float32 [1024], replicated
Inputs may be any that keep to these rules, and one draw needn't show every extreme that they name: Item i's valid slots are its first lengths[i] + 25; every draw has an item of length 475 and one of length 0.
All inputs are finite; a program needn't handle non-finite values.
Results may differ from a plain program's by a relative error of at most 0.02.
Values may be sent and summed in bfloat16 or wider, within the bound.
A program may use at most 256 MiB of HBM per device.

v0:
```python
import jax
import jax.numpy as jnp
from jax import lax
from jax.sharding import PartitionSpec as P

HEAD_DIM = 64
BLOCK = 25
norm_eps = 1e-05
neg_large = -1e30


def layer_norm(values, gain, shift):
    center = values - jnp.mean(values, axis=-1, keepdims=True)
    spread = lax.rsqrt(jnp.mean(center * center, axis=-1, keepdims=True) + norm_eps)
    return center * spread * gain + shift


def exact_gelu(values):
    return jax.nn.gelu(values, approximate=False)


def split_heads(rows):
    return rows.reshape(rows.shape[0], rows.shape[1] // HEAD_DIM, HEAD_DIM)


def item_scores(queries, keys, key_valid):
    scores = jnp.einsum(
        "qhd,khd->hqk", split_heads(queries), split_heads(keys), preferred_element_type=jnp.float32
    ) * HEAD_DIM ** (-0.5)
    return jnp.where(key_valid[None, None, :], scores, neg_large)


def attend_forward(queries, keys, values, key_valid):
    masked = item_scores(queries, keys, key_valid)
    row_max = jnp.max(masked, axis=-1, keepdims=True)
    exp_scores = jnp.exp(masked - row_max)
    row_total = jnp.sum(exp_scores, axis=-1, keepdims=True)
    soft = (exp_scores / row_total).astype(jnp.bfloat16)
    mixed = jnp.einsum(
        "hqk,khd->qhd", soft, split_heads(values), preferred_element_type=jnp.float32
    )
    log_total = row_max[:, :, 0] + jnp.log(row_total[:, :, 0])
    return (mixed.reshape(queries.shape).astype(jnp.bfloat16), log_total)


def attend_backward(queries, keys, values, key_valid, log_total, grad_mixed):
    masked = item_scores(queries, keys, key_valid)
    soft = jnp.exp(masked - log_total[:, :, None])
    grad_heads = split_heads(grad_mixed)
    grad_value = jnp.einsum(
        "hqk,qhd->khd", soft.astype(jnp.bfloat16), grad_heads, preferred_element_type=jnp.float32
    )
    grad_soft = jnp.einsum(
        "qhd,khd->hqk", grad_heads, split_heads(values), preferred_element_type=jnp.float32
    )
    grad_scores = soft * (grad_soft - jnp.sum(soft * grad_soft, axis=-1, keepdims=True))
    scores_low = grad_scores.astype(jnp.bfloat16)
    scale = HEAD_DIM ** (-0.5)
    grad_query = scale * jnp.einsum(
        "hqk,khd->qhd", scores_low, split_heads(keys), preferred_element_type=jnp.float32
    )
    grad_key = scale * jnp.einsum(
        "hqk,qhd->khd", scores_low, split_heads(queries), preferred_element_type=jnp.float32
    )
    return tuple(
        (
            grad.reshape(queries.shape).astype(jnp.bfloat16)
            for grad in (grad_query, grad_key, grad_value)
        )
    )


def per_item(fn, item_count, slot_count, *arrays):
    if item_count == 1:
        return fn(*[a[0] for a in arrays])
    outs = lax.map(lambda packed: fn(*packed), arrays)
    return outs


def local(
    tokens,
    time_embed,
    lengths,
    cotangent,
    w_query,
    w_key,
    w_value,
    w_out,
    w_time,
    w_in,
    w_down,
    b_query,
    b_value,
    b_out,
    b_time,
    b_in,
    b_down,
    gain_one,
    shift_one,
    gain_two,
    shift_two,
):
    f32, bf16 = (jnp.float32, jnp.bfloat16)
    seq_rank = lax.axis_index("seq")
    item_count = time_embed.shape[0]
    token_count = tokens.shape[0]
    slot_count = token_count // item_count
    width = tokens.shape[1]
    rows = w_time.shape[0]

    def mm(a, b, dims):
        return lax.dot_general(a, b, (dims, ((), ())), preferred_element_type=f32)

    def gather(a):
        return lax.all_gather(a, "seq", axis=0, tiled=True)

    def scatter_sum(a):
        return lax.psum_scatter(a, "seq", scatter_dimension=0, tiled=True)

    full_time, full_query, full_key, full_value, full_out = (
        gather(w_time),
        gather(w_query),
        gather(w_key),
        gather(w_value),
        gather(w_out),
    )
    own_lengths = lax.dynamic_slice_in_dim(lengths, seq_rank * item_count, item_count, 0)
    slot_index = lax.broadcasted_iota(jnp.int32, (item_count, slot_count), 1)
    own_valid = slot_index < own_lengths[:, None] + BLOCK
    row_keep = own_valid.reshape(token_count, 1).astype(f32)
    time_proj = mm(time_embed, full_time, ((1,), (0,))) + b_time.astype(f32)
    resid = (tokens.reshape(item_count, slot_count, width) + time_proj[:, None, :]).reshape(
        token_count, width
    )
    resid_low = resid.astype(bf16)
    query_rows = (mm(resid_low, full_query, ((1,), (0,))) + b_query.astype(f32)).astype(bf16)
    key_rows = mm(resid_low, full_key, ((1,), (0,))).astype(bf16)
    value_rows = (mm(resid_low, full_value, ((1,), (0,))) + b_value.astype(f32)).astype(bf16)

    def split_items(a):
        return a.reshape(item_count, slot_count, -1)

    qkv = [split_items(a) for a in (query_rows, key_rows, value_rows)]
    mixed, log_total = per_item(attend_forward, item_count, slot_count, *qkv, own_valid)
    mixed_rows = mixed.reshape(token_count, width)
    attn_out = mm(mixed_rows, full_out, ((1,), (0,))) + b_out.astype(f32)
    first_norm, first_pull = jax.vjp(
        layer_norm, resid + attn_out, gain_one.astype(f32), shift_one.astype(f32)
    )
    first_group = gather(first_norm.astype(bf16))
    bias_in = lax.dynamic_slice_in_dim(b_in, seq_rank * w_in.shape[0], w_in.shape[0], 0)
    hidden_pre = mm(first_group, w_in, ((1,), (1,))) + bias_in.astype(f32)
    hidden, gelu_pull = jax.vjp(exact_gelu, hidden_pre)
    hidden_low = hidden.astype(bf16)
    ffn_part = mm(hidden_low, w_down, ((1,), (0,))).astype(bf16)
    ffn_out = scatter_sum(ffn_part).astype(f32) + b_down.astype(f32)
    second_norm, second_pull = jax.vjp(
        layer_norm, first_norm + ffn_out, gain_two.astype(f32), shift_two.astype(f32)
    )
    layer_out = (second_norm * row_keep).astype(bf16)
    grad_second_in, grad_gain_two, grad_shift_two = second_pull(cotangent.astype(f32) * row_keep)
    grad_ffn = grad_second_in.astype(bf16)
    grad_group = gather(grad_ffn)
    grad_hidden = mm(grad_group, w_down, ((1,), (1,)))
    grad_pre = gelu_pull(grad_hidden)[0].astype(bf16)
    back_part = mm(grad_pre, w_in, ((1,), (0,))).astype(bf16)
    grad_first = grad_second_in + scatter_sum(back_part).astype(f32)
    term_in = mm(grad_pre, first_group, ((0,), (0,))).astype(bf16)
    term_down = mm(hidden_low, grad_group, ((0,), (0,))).astype(bf16)
    sum_ffn = lax.psum(jnp.concatenate([term_in, term_down], axis=0), "dp").astype(f32)
    grad_first_in, grad_gain_one, grad_shift_one = first_pull(grad_first)
    grad_attn = grad_first_in.astype(bf16)
    grad_mixed = mm(grad_attn, full_out, ((1,), (1,))).astype(bf16)
    if item_count == 1:
        extra = (log_total[None], split_items(grad_mixed))
    else:
        extra = (log_total, split_items(grad_mixed))
    grad_query, grad_key, grad_value = (
        a.reshape(token_count, width)
        for a in per_item(attend_backward, item_count, slot_count, *qkv, own_valid, *extra)
    )
    grad_resid = (
        grad_first_in
        + mm(grad_query, full_query, ((1,), (1,)))
        + mm(grad_key, full_key, ((1,), (1,)))
        + mm(grad_value, full_value, ((1,), (1,)))
    )
    grad_tokens = grad_resid.astype(bf16)
    grad_time = jnp.sum(grad_resid.reshape(item_count, slot_count, width), axis=1).astype(bf16)
    terms = [
        mm(resid_low, grad_query, ((0,), (0,))),
        mm(resid_low, grad_key, ((0,), (0,))),
        mm(resid_low, grad_value, ((0,), (0,))),
        mm(mixed_rows, grad_attn, ((0,), (0,))),
    ]
    group = w_out.shape[0]
    stacked = jnp.stack([t.astype(bf16).reshape(-1, group, width) for t in terms], axis=1)
    share = scatter_sum(stacked.reshape(-1, width))
    sum_attn = lax.psum(share, "dp").astype(f32)
    small = jnp.concatenate(
        [
            jnp.stack(
                [
                    jnp.sum(grad_query, axis=0, dtype=f32),
                    jnp.sum(grad_value, axis=0, dtype=f32),
                    jnp.sum(grad_attn, axis=0, dtype=f32),
                    jnp.sum(grad_ffn, axis=0, dtype=f32),
                    grad_gain_one,
                    grad_shift_one,
                    grad_gain_two,
                    grad_shift_two,
                ]
            ).astype(bf16),
            jnp.sum(grad_pre, axis=0, dtype=f32).reshape(-1, width).astype(bf16),
            time_embed,
            grad_time,
        ],
        axis=0,
    )
    every = lax.all_gather(small, ("dp", "seq"), axis=0)
    vectors = jnp.sum(every[:, :8], axis=0, dtype=f32)
    hidden_rows = every.shape[1] - 8 - 2 * item_count
    in_parts = every[:, 8 : 8 + hidden_rows].reshape(-1, b_in.shape[0])
    grad_b_in = jnp.sum(in_parts, axis=0, dtype=f32)
    time_rows = every[:, 8 + hidden_rows : 8 + hidden_rows + item_count].reshape(-1, width)
    time_grads = every[:, 8 + hidden_rows + item_count :].reshape(-1, width)
    own_columns = lax.dynamic_slice_in_dim(time_rows, seq_rank * rows, rows, 1)
    grad_w_time = mm(own_columns, time_grads, ((0,), (0,)))
    grad_b_time = jnp.sum(time_grads, axis=0, dtype=f32)
    return (
        layer_out,
        grad_tokens,
        sum_attn[:group],
        sum_attn[group : 2 * group],
        sum_attn[2 * group : 3 * group],
        sum_attn[3 * group :],
        grad_w_time,
        sum_ffn[: w_in.shape[0]],
        sum_ffn[w_in.shape[0] :],
        vectors[0],
        vectors[1],
        vectors[2],
        grad_b_time,
        grad_b_in,
        vectors[3],
        vectors[4],
        vectors[5],
        vectors[6],
        vectors[7],
    )


def solution(mesh):
    in_specs = (
        P(("dp", "seq"), None),
        P(("dp", "seq"), None),
        P("dp"),
        P(("dp", "seq"), None),
        P("seq", None),
        P("seq", None),
        P("seq", None),
        P("seq", None),
        P("seq", None),
        P("seq", None),
        P("seq", None),
        P(),
        P(),
        P(),
        P(),
        P(),
        P(),
        P(),
        P(),
        P(),
        P(),
    )
    out_specs = (
        P(("dp", "seq"), None),
        P(("dp", "seq"), None),
        P("seq", None),
        P("seq", None),
        P("seq", None),
        P("seq", None),
        P("seq", None),
        P("seq", None),
        P("seq", None),
        P(),
        P(),
        P(),
        P(),
        P(),
        P(),
        P(),
        P(),
        P(),
        P(),
    )
    return jax.shard_map(local, mesh=mesh, in_specs=in_specs, out_specs=out_specs, check_vma=False)
```

profile of v0, /device:TPU:0, one launch (start us, length us, event | category | flops | bytes accessed | tf_op | source)
XLA Modules:
  0.0 732.2 jit_solution(3286179977434555433)
XLA Ops:
  16.0 18.9 %all-gather.10.cloned.1.call-done = bf16[1024,1024]{1,0:T(8,128)(2,1)} async-done(((bf16[256,1024]{1,0:T(8,128)(2,1)}), bf16[1024,1024]{1,0:T(8,128)(2,1)}) %all-gather.10.cloned.1.call-update) | async-done | bytes 2097168 | tf_op jit(solution)/shard_map/all_gather | solution.py:115
  36.9 22.1 %all-gather.14.cloned.1.call-done = bf16[1024,1024]{1,0:T(8,128)(2,1)} async-done(((bf16[256,1024]{1,0:T(8,128)(2,1)}), bf16[1024,1024]{1,0:T(8,128)(2,1)}) %all-gather.14.cloned.1.call-update) | async-done | bytes 2097168 | tf_op jit(solution)/shard_map/all_gather | solution.py:115
  59.1 3.2 add_convert_fusion.1
  63.6 19.7 %all-gather.16.cloned.1.call-done = bf16[1024,1024]{1,0:T(8,128)(2,1)} async-done(((bf16[256,1024]{1,0:T(8,128)(2,1)}), bf16[1024,1024]{1,0:T(8,128)(2,1)}) %all-gather.16.cloned.1.call-update) | async-done | bytes 2097168 | tf_op jit(solution)/shard_map/all_gather | solution.py:115
  83.2 4.1 convolution_convert_fusion.9
  88.9 9.2 %fusion.46 = (f32[16,512]{1,0:T(8,128)S(1)}, f32[16,512,512]{1,2,0:T(8,128)}) fusion(bf16[512,16,64]{0,2,1:T(8,128)(2,1)} %bitcast.89, bf16[512,16,64]{0,2,1:T(8,128)(2,1)S(1)} %bitcast.87, pred[512]{0:T(512)(128)(4,1)S(1)} %iota_compare_fusion), kind=kOutput, calls=%fused_computation.107 | convolution fusion | flops 549445632 | bytes 18907648 | tf_op jit(solution)/shard_map/qhd,khd->hqk/dot_general | solution.py:27
  98.0 9.2 %all-gather.12.cloned.1.call-done = bf16[1024,1024]{1,0:T(8,128)(2,1)} async-done(((bf16[256,1024]{1,0:T(8,128)(2,1)}), bf16[1024,1024]{1,0:T(8,128)(2,1)}) %all-gather.12.cloned.1.call-update) | async-done | bytes 2097168 | tf_op jit(solution)/shard_map/all_gather | solution.py:115
  107.2 4.1 add_convert_fusion.2
  112.9 9.4 %fusion = f32[16,512]{1,0:T(8,128)S(1)} fusion(f32[16,512,512]{1,2,0:T(8,128)} %get-tuple-element.61, f32[16,512]{1,0:T(8,128)S(1)} %get-tuple-element.60), kind=kLoop, calls=%fused_computation.6 | loop fusion | flops 8380416 | bytes 16842752 | tf_op jit(solution)/shard_map/reduce_sum | solution.py:37
  122.2 8.5 %fusion.16 = bf16[16,64,512]{2,1,0:T(8,128)(2,1)} fusion(bf16[512,16,64]{0,2,1:T(8,128)(2,1)S(1)} %bitcast.93, f32[16,512,512]{1,2,0:T(8,128)} %get-tuple-element.61, f32[16,512]{1,0:T(8,128)S(1)} %fusion, f32[16,512]{1,0:T(8,128)S(1)} %get-tuple-element.60), kind=kOutput, calls=%fused_computation.64 | convolution fusion | flops 549978112 | bytes 18939904 | tf_op jit(solution)/shard_map/hqk,khd->qhd/dot_general | solution.py:39
  131.2 3.6 fusion.47
  138.5 33.7 %all-gather.20.cloned.1.call-done = bf16[2048,1024]{1,0:T(8,128)(2,1)} async-done(((bf16[512,1024]{1,0:T(8,128)(2,1)}), bf16[2048,1024]{1,0:T(8,128)(2,1)}) %all-gather.20.cloned.1.call-update) | async-done | bytes 4194320 | tf_op jit(solution)/shard_map/all_gather | solution.py:115
  172.1 25.7 %multiply_convert_fusion.1 = (bf16[2048,1024]{1,0:T(8,128)(2,1)S(1)}, f32[2048,1024]{1,0:T(8,128)}, f32[2048,1024]{1,0:T(8,128)}) fusion(f32[1024]{0:T(1024)S(1)} %dynamic-slice_convert_fusion, bf16[2048,1024]{1,0:T(8,128)(2,1)} %all-gather.20.cloned.1.call-done, bf16[1024,1024]{1,0:T(8,128)(2,1)S(1)} %copy-done), kind=kOutput, calls=%fused_computation.14 | convolution fusion | flops 4433379328 | bytes 27267072 | tf_op jit(solution)/shard_map/dot_general | solution.py:112
  199.8 6.0 convolution_convert_fusion.1
  206.6 44.0 %reduce-scatter.4.cloned.1.call-done = bf16[512,1024]{1,0:T(8,128)(2,1)} async-done(((bf16[2048,1024]{1,0:T(8,128)(2,1)}), bf16[512,1024]{1,0:T(8,128)(2,1)}) %reduce-scatter.4.cloned.1.call-update) | async-done | bytes 1048592 | tf_op jit(solution)/shard_map/reduce_scatter | solution.py:118
  259.6 34.2 %all-gather.22.cloned.1.call-done = bf16[2048,1024]{1,0:T(8,128)(2,1)} async-done(((bf16[512,1024]{1,0:T(8,128)(2,1)}), bf16[2048,1024]{1,0:T(8,128)(2,1)}) %all-gather.22.cloned.1.call-update) | async-done | bytes 4194320 | tf_op jit(solution)/shard_map/all_gather | solution.py:115
  293.8 13.3 %fusion.34 = (bf16[1024]{0:T(1024)(128)(2,1)S(1)}, bf16[2048,1024]{1,0:T(8,128)(2,1)S(1)}) fusion(f32[2048,1024]{1,0:T(8,128)} %get-tuple-element.40, f32[2048,1024]{1,0:T(8,128)} %get-tuple-element.64, f32[1024]{0:T(1024)S(1)} %dynamic-slice_convert_fusion, bf16[2048,1024]{1,0:T(8,128)(2,1)} %all-gather.22.cloned.1.call-done, bf16[1024,1024]{1,0:T(8,128)(2,1)} %param.31), kind=kOutput, calls=%fused_computation.96 | convolution fusion | flops 4328520704 | bytes 27269120 | tf_op jit(solution)/shard_map/dot_general | solution.py:112
  309.1 6.0 convolution_convert_fusion
  315.2 44.7 %reduce-scatter.6.cloned.1.call-done = bf16[512,1024]{1,0:T(8,128)(2,1)} async-done(((bf16[2048,1024]{1,0:T(8,128)(2,1)}), bf16[512,1024]{1,0:T(8,128)(2,1)}) %reduce-scatter.6.cloned.1.call-update) | async-done | bytes 1048592 | tf_op jit(solution)/shard_map/reduce_scatter | solution.py:118
  359.8 3.7 multiply_reduce_fusion.2
  370.2 11.4 %multiply_reduce_fusion = (f32[16,512]{1,0:T(8,128)S(1)}, f32[16,512,512]{1,2,0:T(8,128)}) fusion(f32[16,512,512]{1,2,0:T(8,128)} %get-tuple-element.61, f32[16,512]{1,0:T(8,128)S(1)} %log_add_fusion, bf16[512,16,64]{0,2,1:T(8,128)(2,1)S(1)} %bitcast.91, bf16[512,16,64]{0,2,1:T(8,128)(2,1)} %bitcast.94), kind=kOutput, calls=%fused_computation.1 | convolution fusion | flops 549445632 | bytes 35717120 | tf_op jit(solution)/shard_map/qhd,khd->hqk/dot_general | solution.py:53
  381.6 12.0 %multiply_convert_fusion = bf16[16,512,512]{1,2,0:T(8,128)(2,1)S(1)} fusion(f32[16,512,512]{1,2,0:T(8,128)} %get-tuple-element.66, f32[16,512,512]{1,2,0:T(8,128)} %get-tuple-element.61, f32[16,512]{1,0:T(8,128)S(1)} %get-tuple-element.65, f32[16,512]{1,0:T(8,128)S(1)} %log_add_fusion), kind=kLoop, calls=%fused_computation | loop fusion | flops 16777216 | bytes 42008576 | tf_op jit(solution)/shard_map/convert_element_type | solution.py:57
  399.1 8.6 %bitcast_reduce_fusion = (bf16[16,64]{1,0:T(8,128)(2,1)S(1)}, bf16[16,64,512]{2,1,0:T(8,128)(2,1)S(1)}) fusion(bf16[512,16,64]{0,2,1:T(8,128)(2,1)S(1)} %bitcast.92, f32[16,512,512]{1,2,0:T(8,128)} %get-tuple-element.61, f32[16,512]{1,0:T(8,128)S(1)} %log_add_fusion), kind=kOutput, calls=%fused_computation.68 | convolution fusion | flops 546307072 | bytes 18909184 | tf_op jit(solution)/shard_map/hqk,qhd->khd/dot_general | solution.py:50
  411.8 3.8 pad_maximum_fusion
  415.6 7.9 %copy.79 = bf16[4,4,256,1024]{3,2,1,0:T(8,128)(2,1)} copy(bf16[4,4,256,1024]{3,2,0,1:T(8,128)(2,1)} %pad_maximum_fusion) | data formatting | bytes 16777216 | tf_op jit(solution)/shard_map/stack | solution.py:197
  423.9 8.2 %convolution_convert_fusion.2 = bf16[1024,1024]{1,0:T(8,128)(2,1)S(1)} fusion(bf16[2048,1024]{1,0:T(8,128)(2,1)} %copy-done.36, bf16[2048,1024]{1,0:T(8,128)(2,1)} %all-gather.22.cloned.1.call-done), kind=kOutput, calls=%fused_computation.57 | convolution fusion | flops 4296015872 | bytes 10485760 | tf_op jit(solution)/shard_map/dot_general | solution.py:112
  432.1 4.8 convolution_convert_fusion.3
  439.3 55.8 %reduce-scatter.8.cloned.1.call-done = bf16[1024,1024]{1,0:T(8,128)(2,1)} async-done(((bf16[4096,1024]{1,0:T(8,128)(2,1)}), bf16[1024,1024]{1,0:T(8,128)(2,1)}) %reduce-scatter.8.cloned.1.call-update) | async-done | bytes 2097168 | tf_op jit(solution)/shard_map/reduce_scatter | solution.py:118
  495.2 3.0 fusion.48
  503.7 51.7 %all-gather.1 = bf16[32,11,1024]{2,1,0:T(8,128)(2,1)S(1)} all-gather(bf16[1,11,1024]{2,1,0:T(8,128)(2,1)S(1)} %bitcast.107), channel_id=2, replica_groups=mesh['dp'=8,'seq'=4] {'dp','seq'}, dimensions={0}, use_global_device_ids=true | all-gather | bytes 743424 | tf_op jit(solution)/shard_map/all_gather | solution.py:220
  559.3 156.8 %all-reduce.3.cloned.1.call-done = (bf16[1024,1024]{1,0:T(8,128)(2,1)}, bf16[2048,1024]{1,0:T(8,128)(2,1)}) async-done(((bf16[1024,1024]{1,0:T(8,128)(2,1)}, bf16[2048,1024]{1,0:T(8,128)(2,1)}), (bf16[1024,1024]{1,0:T(8,128)(2,1)}, bf16[2048,1024]{1,0:T(8,128)(2,1)})) %all-reduce.3.cloned.1.call-update) | async-done | bytes 6291472 | tf_op jit(solution)/shard_map/psum | solution.py:199
  716.2 6.8 fusion.41
  (168 shorter events, 62.5 us)
Async XLA Ops:
  7.2 164.9 %copy-start = (bf16[1024,1024]{1,0:T(8,128)(2,1)S(1)}, bf16[1024,1024]{1,0:T(8,128)(2,1)}, u32[]{:S(2)}) copy-start(bf16[1024,1024]{1,0:T(8,128)(2,1)} %param.30) | copy-start | bytes 6291460
  7.2 29.7 %copy-start.28 = (bf16[1024]{0:T(1024)(128)(2,1)S(1)}, bf16[1024]{0:T(1024)(128)(2,1)}, u32[]{:S(2)}) copy-start(bf16[1024]{0:T(1024)(128)(2,1)} %param.35) | copy-start | bytes 6148
  7.2 27.7 %all-gather.10.cloned.1.call-start = ((), (), s32[]{:S(2)}) async-start(), calls=%async_computation.3 | async-start | bytes 2621440 | tf_op jit(solution)/shard_map/all_gather | solution.py:115
  7.9 51.1 %all-gather.14.cloned.1.call-start = ((), (), s32[]{:S(2)}) async-start(), calls=%async_computation.5 | async-start | bytes 2621440 | tf_op jit(solution)/shard_map/all_gather | solution.py:115
  8.7 74.5 %all-gather.16.cloned.1.call-start = ((), (), s32[]{:S(2)}) async-start(), calls=%async_computation.6 | async-start | bytes 2621440 | tf_op jit(solution)/shard_map/all_gather | solution.py:115
  9.4 97.8 %all-gather.12.cloned.1.call-start = ((), (), s32[]{:S(2)}) async-start(), calls=%async_computation.4 | async-start | bytes 2621440 | tf_op jit(solution)/shard_map/all_gather | solution.py:115
  10.0 121.2 %all-gather.18.cloned.1.call-start = ((), (), s32[]{:S(2)}) async-start(), calls=%async_computation.7 | async-start | bytes 2621440 | tf_op jit(solution)/shard_map/all_gather | solution.py:115
  10.6 161.5 %all-gather.20.cloned.1.call-start = ((), (), s32[]{:S(2)}) async-start(), calls=%async_computation.8 | async-start | bytes 5242880 | tf_op jit(solution)/shard_map/all_gather | solution.py:115
  36.9 94.3 %copy-start.25 = (f32[1024]{0:T(1024)}, f32[1024]{0:T(1024)S(1)}, u32[]{:S(2)}) copy-start(f32[1024]{0:T(1024)S(1)} %convert_add_fusion.2) | copy-start | bytes 12292
  88.9 9.2 %copy-start.5 = (bf16[512,1024]{0,1:T(8,128)(2,1)}, bf16[512,1024]{0,1:T(8,128)(2,1)S(1)}, u32[]{:S(2)}) copy-start(bf16[512,1024]{0,1:T(8,128)(2,1)S(1)} %copy.73) | copy-start | bytes 3145732
  112.9 9.4 %copy-start.11 = (bf16[512,1024]{0,1:T(8,128)(2,1)}, bf16[512,1024]{0,1:T(8,128)(2,1)S(1)}, u32[]{:S(2)}) copy-start(bf16[512,1024]{0,1:T(8,128)(2,1)S(1)} %copy.71) | copy-start | bytes 3145732
  137.5 113.1 %reduce-scatter.4.cloned.1.call-start = ((), (), s32[]{:S(2)}) async-start(), calls=%async_computation.9 | async-start | bytes 5242880 | tf_op jit(solution)/shard_map/reduce_scatter | solution.py:118
  172.1 27.7 %copy-start.33 = (bf16[1024,1024]{1,0:T(8,128)(2,1)S(1)}, bf16[1024,1024]{1,0:T(8,128)(2,1)}, u32[]{:S(2)}) copy-start(bf16[1024,1024]{1,0:T(8,128)(2,1)} %param.31) | copy-start | bytes 6291460
  205.9 47.8 %copy-start.12 = (bf16[512,1024]{1,0:T(8,128)(2,1)S(1)}, bf16[512,1024]{1,0:T(8,128)(2,1)}, u32[]{:S(2)}) copy-start(bf16[512,1024]{1,0:T(8,128)(2,1)} %param.24) | copy-start | bytes 3145732
  205.9 87.9 %all-gather.22.cloned.1.call-start = ((), (), s32[]{:S(2)}) async-start(), calls=%async_computation.10 | async-start | bytes 5242880 | tf_op jit(solution)/shard_map/all_gather | solution.py:115
  259.2 100.6 %reduce-scatter.6.cloned.1.call-start = ((), (), s32[]{:S(2)}) async-start(), calls=%async_computation.11 | async-start | bytes 5242880 | tf_op jit(solution)/shard_map/reduce_scatter | solution.py:118
  315.1 180.0 %reduce-scatter.8.cloned.1.call-start = ((), (), s32[]{:S(2)}) async-start(), calls=%async_computation.12 | async-start | bytes 10485760 | tf_op jit(solution)/shard_map/reduce_scatter | solution.py:118
  359.8 3.7 copy-start.2
  359.8 3.8 copy-start.4
  359.8 4.0 copy-start.13
  381.6 12.0 %copy-start.6 = (bf16[512,1024]{0,1:T(8,128)(2,1)S(1)}, bf16[512,1024]{0,1:T(8,128)(2,1)}, u32[]{:S(2)}) copy-start(bf16[512,1024]{0,1:T(8,128)(2,1)} %copy-done.5) | copy-start | bytes 3145732
  395.2 12.6 %copy-start.14 = (bf16[16,64,512]{2,1,0:T(8,128)(2,1)}, bf16[16,64,512]{2,1,0:T(8,128)(2,1)S(1)}, u32[]{:S(2)}) copy-start(bf16[16,64,512]{2,1,0:T(8,128)(2,1)S(1)} %get-tuple-element.69) | copy-start | bytes 3145732
  397.8 11.3 %copy-start.17 = (bf16[16,64,512]{2,1,0:T(8,128)(2,1)}, bf16[16,64,512]{2,1,0:T(8,128)(2,1)S(1)}, u32[]{:S(2)}) copy-start(bf16[16,64,512]{2,1,0:T(8,128)(2,1)S(1)} %multiply_convert_fusion.2) | copy-start | bytes 3145732
  399.1 8.7 %copy-start.21 = (bf16[512,1024]{1,0:T(8,128)(2,1)S(1)}, bf16[512,1024]{1,0:T(8,128)(2,1)}, u32[]{:S(2)}) copy-start(bf16[512,1024]{1,0:T(8,128)(2,1)} %param.21) | copy-start | bytes 3145732
  399.1 8.7 %copy-start.26 = (f32[1024]{0:T(1024)S(1)}, f32[1024]{0:T(1024)}, u32[]{:S(2)}) copy-start(f32[1024]{0:T(1024)} %copy-done.25) | copy-start | bytes 12292
  423.6 292.6 %all-reduce.3.cloned.1.call-start = ((), (), s32[]{:S(2)}) async-start(), calls=%async_computation.13 | async-start | bytes 12582912 | tf_op jit(solution)/shard_map/psum | solution.py:199
  423.8 8.2 %copy-start.32 = (bf16[2048,1024]{1,0:T(8,128)(2,1)S(1)}, bf16[2048,1024]{1,0:T(8,128)(2,1)}, u32[]{:S(2)}) copy-start(bf16[2048,1024]{1,0:T(8,128)(2,1)} %all-gather.20.cloned.1.call-done) | copy-start | bytes 12582916
  423.8 8.2 %copy-start.38 = (bf16[2048,1024]{1,0:T(8,128)(2,1)S(1)}, bf16[2048,1024]{1,0:T(8,128)(2,1)}, u32[]{:S(2)}) copy-start(bf16[2048,1024]{1,0:T(8,128)(2,1)} %copy-done.37) | copy-start | bytes 12582916
  439.3 55.9 %copy-start.15 = (bf16[16,64,512]{2,1,0:T(8,128)(2,1)S(1)}, bf16[16,64,512]{2,1,0:T(8,128)(2,1)}, u32[]{:S(2)}) copy-start(bf16[16,64,512]{2,1,0:T(8,128)(2,1)} %copy-done.14) | copy-start | bytes 3145732
  495.2 3.1 copy-start.18
  495.2 3.1 copy-start.34
  716.2 6.8 copy-start.10
  (18 other events, 32.2 us)
Sparse Core Ops, SparseCore 0:
  9.6 25.2 all-gather.9
  36.5 22.5 all-gather.13
  60.6 22.5 all-gather.15
  84.6 22.5 all-gather.11
  108.6 22.5 all-gather.17
  137.6 34.4 all-gather.19
  206.0 44.5 reduce-scatter.3
  259.3 34.4 all-gather.21
  315.2 44.5 reduce-scatter.5
  423.7 71.3 reduce-scatter.7
  499.6 216.4 all-reduce.2
where the time goes:
time: 741 us; the launch traced here: 732 us
  waiting for transfers between devices  443 us (60%)
  matrix products  138 us (19%)
  blocking collectives  51.7 us (7%)
  other arithmetic  47.2 us (6%)
  local copies, waits for them, and re-layouts  35.2 us (5%)
  between operations  15.6 us (2%)
    psum x1, waiting for transfers between devices, local(): sum_attn = lax.psum(share, 'dp').astype(f32)  157 us
    reduce_scatter x3, waiting for transfers between devices, scatter_sum(): return lax.psum_scatter(a, 'seq', scatter_dimension=0, tiled=True)  145 us
    all_gather x7, waiting for transfers between devices, gather(): return lax.all_gather(a, 'seq', axis=0, tiled=True)  138 us
    dot_general x20, matrix products, mm(): return lax.dot_general(a, b, (dims, ((), ())), preferred_element_type=f32)  96.6 us
    all_gather x1, blocking collectives, local(): every = lax.all_gather(small, ('dp', 'seq'), axis=0)  51.7 us
  transfers between devices with their start and end apart: 11, of which 11 were waited for; matrix products, arithmetic and copies ran while one was open for 10% of the time, Pallas kernels for 0%

commit v1 on v0

--- a/solution.py
+++ b/solution.py
@@ -7,6 +7,18 @@
 BLOCK = 25
 norm_eps = 1e-05
 neg_large = -1e30
+
+
+def collect(x, axis, dim):
+    ways, here, step = (lax.axis_size(axis), lax.axis_index(axis), x.shape[dim])
+    line, have = (x, 1)
+    while have < ways:
+        line = jnp.concatenate(
+            [line, lax.ppermute(line, axis, [(d, (d - have) % ways) for d in range(ways)])],
+            axis=dim,
+        )
+        have = 2 * have
+    return jnp.roll(line, here * step, axis=dim)
 
 
 def layer_norm(values, gain, shift):
@@ -112,7 +124,7 @@
         return lax.dot_general(a, b, (dims, ((), ())), preferred_element_type=f32)
 
     def gather(a):
-        return lax.all_gather(a, "seq", axis=0, tiled=True)
+        return collect(a, "seq", 0)
 
     def scatter_sum(a):
         return lax.psum_scatter(a, "seq", scatter_dimension=0, tiled=True)

time: 741 us -> 888 us (1.20)
  waiting for transfers between devices: 443 us -> 513 us
  other arithmetic: 47.2 us -> 113 us
  starting transfers between devices: 1.27 us -> 12.5 us
    ppermute x0 -> x14, waiting for transfers between devices: none -> 209 us  [collect(): lax.ppermute(line, axis, [(d, (d - have) % ways) for d in range(ways)])]
    all_gather x7 -> x0, waiting for transfers between devices: 138 us -> none  [gather(): return lax.all_gather(a, 'seq', axis=0, tiled=True)]
    concatenate x0 -> x13, other arithmetic: none -> 68.3 us  [the longest x6 56.9 us: collect(): return jnp.roll(line, here * step, axis=dim)]
    ppermute x0 -> x14, starting transfers between devices: none -> 12.1 us  [collect(): lax.ppermute(line, axis, [(d, (d - have) % ways) for d in range(ways)])]
  transfers between devices with their start and end apart: 11 -> 18, of which waited for: 11 -> 14; matrix products, arithmetic and copies ran while one was open for 10% -> 12% of each run, Pallas kernels for 0% -> 0%
where the time goes in v1:
time: 888 us; the launch traced here: 879 us
  waiting for transfers between devices  513 us (58%)
  matrix products  132 us (15%)
  other arithmetic  113 us (13%)
  blocking collectives  51.5 us (6%)
  local copies, waits for them, and re-layouts  41.4 us (5%)
  between operations  15.7 us (2%)
  starting transfers between devices  12.5 us (1%)
    ppermute x14, waiting for transfers between devices, collect(): lax.ppermute(line, axis, [(d, (d - have) % ways) for d in range(ways)])  209 us
    psum x1, waiting for transfers between devices, local(): sum_attn = lax.psum(share, 'dp').astype(f32)  157 us
    reduce_scatter x3, waiting for transfers between devices, scatter_sum(): return lax.psum_scatter(a, 'seq', scatter_dimension=0, tiled=True)  148 us
    dot_general x20, matrix products, mm(): return lax.dot_general(a, b, (dims, ((), ())), preferred_element_type=f32)  90.6 us
    concatenate x6, other arithmetic, collect(): return jnp.roll(line, here * step, axis=dim)  56.9 us
    all_gather x1, blocking collectives, local(): every = lax.all_gather(small, ('dp', 'seq'), axis=0)  51.5 us
  transfers between devices with their start and end apart: 18, of which 14 were waited for; matrix products, arithmetic and copies ran while one was open for 12% of the time, Pallas kernels for 0%

profile of v1, /device:TPU:0, one launch (start us, length us, event | category | flops | bytes accessed | tf_op | source)
XLA Modules:
  0.0 878.6 jit_solution(17638638668347512443)
XLA Ops:
  10.4 6.3 collective-permute-done
  30.7 25.5 %collective-permute-done.6 = bf16[256,1024]{1,0:T(8,128)(2,1)} collective-permute-done((bf16[256,1024]{1,0:T(8,128)(2,1)}, bf16[256,1024]{1,0:T(8,128)(2,1)}, u32[]{:S(2)}, u32[]{:S(2)}) %collective-permute-start.6) | collective-permute-done | bytes 524320 | tf_op jit(solution)/shard_map/ppermute | solution.py:17
  58.9 8.6 collective-permute-done.2
  70.1 8.6 collective-permute-done.8
  84.9 17.2 %collective-permute-done.5 = bf16[512,1024]{1,0:T(8,128)(2,1)S(1)} collective-permute-done((bf16[512,1024]{1,0:T(8,128)(2,1)S(1)}, bf16[512,1024]{1,0:T(8,128)(2,1)S(1)}, u32[]{:S(2)}, u32[]{:S(2)}) %collective-permute-start.5) | collective-permute-done | bytes 1048608 | tf_op jit(solution)/shard_map/ppermute | solution.py:17
  102.1 8.1 fusion.34
  116.1 25.3 %collective-permute-done.3 = bf16[512,1024]{1,0:T(8,128)(2,1)} collective-permute-done((bf16[512,1024]{1,0:T(8,128)(2,1)}, bf16[512,1024]{1,0:T(8,128)(2,1)}, u32[]{:S(2)}, u32[]{:S(2)}) %collective-permute-start.3) | collective-permute-done | bytes 1048608 | tf_op jit(solution)/shard_map/ppermute | solution.py:17
  141.4 6.1 fusion.39
  153.4 6.5 fusion.29
  164.9 9.2 %fusion.84 = (f32[16,512]{1,0:T(8,128)S(1)}, f32[16,512,512]{1,2,0:T(8,128)}) fusion(bf16[512,16,64]{0,2,1:T(8,128)(2,1)} %bitcast.88, bf16[512,16,64]{0,2,1:T(8,128)(2,1)S(1)} %bitcast.86, pred[512]{0:T(512)(128)(4,1)S(1)} %iota_compare_fusion), kind=kOutput, calls=%fused_computation.193 | convolution fusion | flops 549445632 | bytes 18907648 | tf_op jit(solution)/shard_map/qhd,khd->hqk/dot_general | solution.py:39
  174.1 8.4 fusion
  182.5 7.6 fusion.53
  190.1 6.5 fusion.24
  199.9 12.3 %collective-permute-done.10 = bf16[512,1024]{1,0:T(8,128)(2,1)S(1)} collective-permute-done((bf16[512,1024]{1,0:T(8,128)(2,1)S(1)}, bf16[512,1024]{1,0:T(8,128)(2,1)S(1)}, u32[]{:S(2)}, u32[]{:S(2)}) %collective-permute-start.10) | collective-permute-done | bytes 1048608 | tf_op jit(solution)/shard_map/ppermute | solution.py:17
  216.9 45.9 %collective-permute-done.11 = bf16[1024,1024]{1,0:T(8,128)(2,1)} collective-permute-done((bf16[1024,1024]{1,0:T(8,128)(2,1)}, bf16[1024,1024]{1,0:T(8,128)(2,1)}, u32[]{:S(2)}, u32[]{:S(2)}) %collective-permute-start.11) | collective-permute-done | bytes 2097184 | tf_op jit(solution)/shard_map/ppermute | solution.py:17
  262.8 11.8 %fusion.19 = bf16[2048,1024]{1,0:T(8,128)(2,1)S(1)} fusion(s32[]{:T(128)S(6)} %select_n.56, bf16[512,1024]{1,0:T(8,128)(2,1)S(1)} %fusion.52, bf16[512,1024]{1,0:T(8,128)(2,1)} %copy-done.19, bf16[1024,1024]{1,0:T(8,128)(2,1)} %collective-permute-done.11), kind=kLoop, calls=%fused_computation.48 | loop fusion | flops 25165824 | bytes 8388612 | tf_op jit(solution)/shard_map/jit(_roll_dynamic)/concatenate | solution.py:21
  274.6 23.7 %multiply_convert_fusion.1 = (bf16[2048,1024]{1,0:T(8,128)(2,1)S(1)}, f32[2048,1024]{1,0:T(8,128)}, f32[2048,1024]{1,0:T(8,128)}) fusion(f32[1024]{0:T(1024)S(1)} %dynamic-slice_convert_fusion, bf16[2048,1024]{1,0:T(8,128)(2,1)S(1)} %fusion.19, bf16[1024,1024]{1,0:T(8,128)(2,1)S(1)} %copy-done), kind=kOutput, calls=%fused_computation.26 | convolution fusion | flops 4433379328 | bytes 27267072 | tf_op jit(solution)/shard_map/dot_general | solution.py:124
  300.3 6.0 convolution_convert_fusion.1
  307.1 45.9 %reduce-scatter.4.cloned.1.call-done = bf16[512,1024]{1,0:T(8,128)(2,1)} async-done(((bf16[2048,1024]{1,0:T(8,128)(2,1)}), bf16[512,1024]{1,0:T(8,128)(2,1)}) %reduce-scatter.4.cloned.1.call-update) | async-done | bytes 1048592 | tf_op jit(solution)/shard_map/reduce_scatter | solution.py:130
  360.7 12.3 %collective-permute-done.12 = bf16[512,1024]{1,0:T(8,128)(2,1)S(1)} collective-permute-done((bf16[512,1024]{1,0:T(8,128)(2,1)S(1)}, bf16[512,1024]{1,0:T(8,128)(2,1)S(1)}, u32[]{:S(2)}, u32[]{:S(2)}) %collective-permute-start.12) | collective-permute-done | bytes 1048608 | tf_op jit(solution)/shard_map/ppermute | solution.py:17
  374.6 46.6 %collective-permute-done.13 = bf16[1024,1024]{1,0:T(8,128)(2,1)S(1)} collective-permute-done((bf16[1024,1024]{1,0:T(8,128)(2,1)S(1)}, bf16[1024,1024]{1,0:T(8,128)(2,1)S(1)}, u32[]{:S(2)}, u32[]{:S(2)}) %collective-permute-start.13) | collective-permute-done | bytes 2097184 | tf_op jit(solution)/shard_map/ppermute | solution.py:17
  421.2 17.8 %fusion.14 = bf16[2048,1024]{1,0:T(8,128)(2,1)S(1)} fusion(s32[]{:T(128)S(6)} %select_n.56, bf16[512,1024]{1,0:T(8,128)(2,1)S(1)} %get-tuple-element.32, bf16[512,1024]{1,0:T(8,128)(2,1)S(1)} %collective-permute-done.12, bf16[1024,1024]{1,0:T(8,128)(2,1)S(1)} %collective-permute-done.13), kind=kLoop, calls=%fused_computation.43 | loop fusion | flops 25165824 | bytes 8388612 | tf_op jit(solution)/shard_map/jit(_roll_dynamic)/concatenate | solution.py:21
  439.0 13.1 %fusion.72 = (bf16[1024]{0:T(1024)(128)(2,1)S(1)}, bf16[2048,1024]{1,0:T(8,128)(2,1)S(1)}) fusion(f32[2048,1024]{1,0:T(8,128)} %get-tuple-element.42, f32[2048,1024]{1,0:T(8,128)} %get-tuple-element.66, f32[1024]{0:T(1024)S(1)} %dynamic-slice_convert_fusion, bf16[2048,1024]{1,0:T(8,128)(2,1)S(1)} %fusion.14, bf16[1024,1024]{1,0:T(8,128)(2,1)S(1)} %copy-done.54), kind=kOutput, calls=%fused_computation.182 | convolution fusion | flops 4328520704 | bytes 27269120 | tf_op jit(solution)/shard_map/dot_general | solution.py:124
  460.2 46.0 %reduce-scatter.6.cloned.1.call-done = bf16[512,1024]{1,0:T(8,128)(2,1)} async-done(((bf16[2048,1024]{1,0:T(8,128)(2,1)}), bf16[512,1024]{1,0:T(8,128)(2,1)}) %reduce-scatter.6.cloned.1.call-update) | async-done | bytes 1048592 | tf_op jit(solution)/shard_map/reduce_scatter | solution.py:130
  518.3 8.6 bitcast_reduce_fusion
  527.0 11.5 %multiply_reduce_fusion = (f32[16,512]{1,0:T(8,128)S(1)}, f32[16,512,512]{1,2,0:T(8,128)}) fusion(f32[16,512,512]{1,2,0:T(8,128)} %get-tuple-element.63, f32[16,512]{1,0:T(8,128)S(1)} %log_add_fusion, bf16[512,16,64]{0,2,1:T(8,128)(2,1)S(1)} %bitcast.91, bf16[512,16,64]{0,2,1:T(8,128)(2,1)S(1)} %bitcast.93), kind=kOutput, calls=%fused_computation.1 | convolution fusion | flops 549445632 | bytes 35717120 | tf_op jit(solution)/shard_map/qhd,khd->hqk/dot_general | solution.py:65
  538.5 11.8 %multiply_convert_fusion = bf16[16,512,512]{1,2,0:T(8,128)(2,1)S(1)} fusion(f32[16,512,512]{1,2,0:T(8,128)} %get-tuple-element.68, f32[16,512,512]{1,2,0:T(8,128)} %get-tuple-element.63, f32[16,512]{1,0:T(8,128)S(1)} %get-tuple-element.67, f32[16,512]{1,0:T(8,128)S(1)} %log_add_fusion), kind=kLoop, calls=%fused_computation | loop fusion | flops 16777216 | bytes 42008576 | tf_op jit(solution)/shard_map/convert_element_type | solution.py:69
  562.8 8.0 copy.79
  570.8 8.2 convolution_convert_fusion.2
  586.3 56.0 %reduce-scatter.8.cloned.1.call-done = bf16[1024,1024]{1,0:T(8,128)(2,1)} async-done(((bf16[4096,1024]{1,0:T(8,128)(2,1)}), bf16[1024,1024]{1,0:T(8,128)(2,1)}) %reduce-scatter.8.cloned.1.call-update) | async-done | bytes 2097168 | tf_op jit(solution)/shard_map/reduce_scatter | solution.py:130
  651.1 51.5 %all-gather.1 = bf16[32,11,1024]{2,1,0:T(8,128)(2,1)S(1)} all-gather(bf16[1,11,1024]{2,1,0:T(8,128)(2,1)S(1)} %bitcast.106), channel_id=2, replica_groups=mesh['dp'=8,'seq'=4] {'dp','seq'}, dimensions={0}, use_global_device_ids=true | all-gather | bytes 743424 | tf_op jit(solution)/shard_map/all_gather | solution.py:232
  706.6 156.8 %all-reduce.3.cloned.1.call-done = (bf16[1024,1024]{1,0:T(8,128)(2,1)}, bf16[2048,1024]{1,0:T(8,128)(2,1)}) async-done(((bf16[1024,1024]{1,0:T(8,128)(2,1)}, bf16[2048,1024]{1,0:T(8,128)(2,1)}), (bf16[1024,1024]{1,0:T(8,128)(2,1)}, bf16[2048,1024]{1,0:T(8,128)(2,1)})) %all-reduce.3.cloned.1.call-update) | async-done | bytes 6291472 | tf_op jit(solution)/shard_map/psum | solution.py:211
  (226 shorter events, 125.3 us)
Async XLA Ops:
  7.2 267.4 %copy-start = (bf16[1024,1024]{1,0:T(8,128)(2,1)S(1)}, bf16[1024,1024]{1,0:T(8,128)(2,1)}, u32[]{:S(2)}) copy-start(bf16[1024,1024]{1,0:T(8,128)(2,1)} %param.34) | copy-start | bytes 6291460
  7.2 49.0 %copy-start.28 = (bf16[256,1024]{1,0:T(8,128)(2,1)S(1)}, bf16[256,1024]{1,0:T(8,128)(2,1)}, u32[]{:S(2)}) copy-start(bf16[256,1024]{1,0:T(8,128)(2,1)} %param.30) | copy-start | bytes 1572868
  7.2 60.2 %copy-start.27 = (bf16[256,1024]{1,0:T(8,128)(2,1)S(1)}, bf16[256,1024]{1,0:T(8,128)(2,1)}, u32[]{:S(2)}) copy-start(bf16[256,1024]{1,0:T(8,128)(2,1)} %param.31) | copy-start | bytes 1572868
  7.2 345.8 %reduce-scatter.4.cloned.1.call-start = ((), (), s32[]{:S(2)}) async-start(), calls=%async_computation.3 | async-start | bytes 5242880 | tf_op jit(solution)/shard_map/reduce_scatter | solution.py:130
  7.3 9.5 %collective-permute-start = (bf16[256,1024]{1,0:T(8,128)(2,1)}, bf16[256,1024]{1,0:T(8,128)(2,1)S(1)}, u32[]{:S(2)}, u32[]{:S(2)}) collective-permute-start(bf16[256,1024]{1,0:T(8,128)(2,1)} %param.33), channel_id=1, source_target_pairs={{0,3},{1,0},{2,1},{3,2},{4,7},{5,4},{6,5},{7,6},{8,11},{9,8},{10,9... | collective-permute-start | bytes 1572872 | tf_op jit(solution)/shard_map/ppermute | solution.py:17
  9.8 19.0 %collective-permute-start.4 = (bf16[256,1024]{1,0:T(8,128)(2,1)}, bf16[256,1024]{1,0:T(8,128)(2,1)}, u32[]{:S(2)}, u32[]{:S(2)}) collective-permute-start(bf16[256,1024]{1,0:T(8,128)(2,1)} %param.29), channel_id=1, source_target_pairs={{0,3},{1,0},{2,1},{3,2},{4,7},{5,4},{6,5},{7,6},{8,11},{9,8},{10,9... | collective-permute-start | bytes 1572872 | tf_op jit(solution)/shard_map/ppermute | solution.py:17
  19.6 61.7 %collective-permute-start.1 = (bf16[512,1024]{1,0:T(8,128)(2,1)}, bf16[512,1024]{1,0:T(8,128)(2,1)}, u32[]{:S(2)}, u32[]{:S(2)}) collective-permute-start(bf16[512,1024]{1,0:T(8,128)(2,1)} %pad_maximum_fusion.4), channel_id=1, source_target_pairs={{0,2},{1,3},{2,0},{3,1},{4,6},{5,7},{6,4},{7,5},{8,10},{9,11},{10,... | collective-permute-start | bytes 3145736 | tf_op jit(solution)/shard_map/ppermute | solution.py:17
  20.2 36.0 %collective-permute-start.6 = (bf16[256,1024]{1,0:T(8,128)(2,1)}, bf16[256,1024]{1,0:T(8,128)(2,1)}, u32[]{:S(2)}, u32[]{:S(2)}) collective-permute-start(bf16[256,1024]{1,0:T(8,128)(2,1)} %param.30), channel_id=1, source_target_pairs={{0,3},{1,0},{2,1},{3,2},{4,7},{5,4},{6,5},{7,6},{8,11},{9,8},{10,9... | collective-permute-start | bytes 1572872 | tf_op jit(solution)/shard_map/ppermute | solution.py:17
  21.7 45.7 %collective-permute-start.2 = (bf16[256,1024]{1,0:T(8,128)(2,1)}, bf16[256,1024]{1,0:T(8,128)(2,1)}, u32[]{:S(2)}, u32[]{:S(2)}) collective-permute-start(bf16[256,1024]{1,0:T(8,128)(2,1)} %param.31), channel_id=1, source_target_pairs={{0,3},{1,0},{2,1},{3,2},{4,7},{5,4},{6,5},{7,6},{8,11},{9,8},{10,9... | collective-permute-start | bytes 1572872 | tf_op jit(solution)/shard_map/ppermute | solution.py:17
  21.8 56.9 %collective-permute-start.8 = (bf16[256,1024]{1,0:T(8,128)(2,1)}, bf16[256,1024]{1,0:T(8,128)(2,1)}, u32[]{:S(2)}, u32[]{:S(2)}) collective-permute-start(bf16[256,1024]{1,0:T(8,128)(2,1)} %param.32), channel_id=1, source_target_pairs={{0,3},{1,0},{2,1},{3,2},{4,7},{5,4},{6,5},{7,6},{8,11},{9,8},{10,9... | collective-permute-start | bytes 1572872 | tf_op jit(solution)/shard_map/ppermute | solution.py:17
  26.7 52.0 %copy-start.29 = (bf16[256,1024]{1,0:T(8,128)(2,1)S(1)}, bf16[256,1024]{1,0:T(8,128)(2,1)}, u32[]{:S(2)}) copy-start(bf16[256,1024]{1,0:T(8,128)(2,1)} %param.32) | copy-start | bytes 1572868
  28.7 52.7 %copy-start.42 = (bf16[256,1024]{1,0:T(8,128)(2,1)S(1)}, bf16[256,1024]{1,0:T(8,128)(2,1)}, u32[]{:S(2)}) copy-start(bf16[256,1024]{1,0:T(8,128)(2,1)} %param.33) | copy-start | bytes 1572868
  28.7 52.6 %copy-start.44 = (bf16[256,1024]{1,0:T(8,128)(2,1)S(1)}, bf16[256,1024]{1,0:T(8,128)(2,1)}, u32[]{:S(2)}) copy-start(bf16[256,1024]{1,0:T(8,128)(2,1)} %copy-done.43) | copy-start | bytes 1572868
  28.7 52.6 %copy-start.47 = (bf16[1,1024]{1,0:T(2,128)(2,1)S(1)}, bf16[1,1024]{1,0:T(2,128)(2,1)}, u32[]{:S(2)}) copy-start(bf16[1,1024]{1,0:T(2,128)(2,1)} %param.26) | copy-start | bytes 6148
  30.1 72.0 %collective-permute-start.5 = (bf16[512,1024]{1,0:T(8,128)(2,1)S(1)}, bf16[512,1024]{1,0:T(8,128)(2,1)S(1)}, u32[]{:S(2)}, u32[]{:S(2)}) collective-permute-start(bf16[512,1024]{1,0:T(8,128)(2,1)S(1)} %pad_maximum_fusion.6), channel_id=1, source_target_pairs={{0,2},{1,3},{2,0},{3,1},{4,6},{5,7},{6,4},{7,5},{8,10},{9,11},{10,... | collective-permute-start | bytes 3145736 | tf_op jit(solution)/shard_map/ppermute | solution.py:17
  58.3 95.1 %collective-permute-start.7 = (bf16[512,1024]{1,0:T(8,128)(2,1)}, bf16[512,1024]{1,0:T(8,128)(2,1)}, u32[]{:S(2)}, u32[]{:S(2)}) collective-permute-start(bf16[512,1024]{1,0:T(8,128)(2,1)} %pad_maximum_fusion.7), channel_id=1, source_target_pairs={{0,2},{1,3},{2,0},{3,1},{4,6},{5,7},{6,4},{7,5},{8,10},{9,11},{10,... | collective-permute-start | bytes 3145736 | tf_op jit(solution)/shard_map/ppermute | solution.py:17
  69.5 71.9 %collective-permute-start.3 = (bf16[512,1024]{1,0:T(8,128)(2,1)}, bf16[512,1024]{1,0:T(8,128)(2,1)}, u32[]{:S(2)}, u32[]{:S(2)}) collective-permute-start(bf16[512,1024]{1,0:T(8,128)(2,1)} %pad_maximum_fusion.5), channel_id=1, source_target_pairs={{0,2},{1,3},{2,0},{3,1},{4,6},{5,7},{6,4},{7,5},{8,10},{9,11},{10,... | collective-permute-start | bytes 3145736 | tf_op jit(solution)/shard_map/ppermute | solution.py:17
  80.8 109.3 %collective-permute-start.9 = (bf16[512,1024]{1,0:T(8,128)(2,1)}, bf16[512,1024]{1,0:T(8,128)(2,1)}, u32[]{:S(2)}, u32[]{:S(2)}) collective-permute-start(bf16[512,1024]{1,0:T(8,128)(2,1)} %pad_maximum_fusion.8), channel_id=1, source_target_pairs={{0,2},{1,3},{2,0},{3,1},{4,6},{5,7},{6,4},{7,5},{8,10},{9,11},{10,... | collective-permute-start | bytes 3145736 | tf_op jit(solution)/shard_map/ppermute | solution.py:17
  84.8 26.7 %copy-start.33 = (bf16[512,1024]{1,0:T(8,128)(2,1)S(1)}, bf16[512,1024]{1,0:T(8,128)(2,1)}, u32[]{:S(2)}) copy-start(bf16[512,1024]{1,0:T(8,128)(2,1)} %param.25) | copy-start | bytes 3145732
  84.9 111.8 %copy-start.45 = (f32[1024]{0:T(1024)}, f32[1024]{0:T(1024)S(1)}, u32[]{:S(2)}) copy-start(f32[1024]{0:T(1024)S(1)} %convert_add_fusion.2) | copy-start | bytes 12292
  116.1 32.8 %copy-start.34 = (bf16[512,1024]{1,0:T(8,128)(2,1)S(1)}, bf16[512,1024]{1,0:T(8,128)(2,1)}, u32[]{:S(2)}) copy-start(bf16[512,1024]{1,0:T(8,128)(2,1)} %param.25) | copy-start | bytes 3145732
  199.8 12.4 %collective-permute-start.10 = (bf16[512,1024]{1,0:T(8,128)(2,1)S(1)}, bf16[512,1024]{1,0:T(8,128)(2,1)S(1)}, u32[]{:S(2)}, u32[]{:S(2)}) collective-permute-start(bf16[512,1024]{1,0:T(8,128)(2,1)S(1)} %fusion.52), channel_id=1, source_target_pairs={{0,3},{1,0},{2,1},{3,2},{4,7},{5,4},{6,5},{7,6},{8,11},{9,8},{10,9... | collective-permute-start | bytes 3145736 | tf_op jit(solution)/shard_map/ppermute | solution.py:17
  214.8 48.0 %collective-permute-start.11 = (bf16[1024,1024]{1,0:T(8,128)(2,1)}, bf16[1024,1024]{1,0:T(8,128)(2,1)}, u32[]{:S(2)}, u32[]{:S(2)}) collective-permute-start(bf16[1024,1024]{1,0:T(8,128)(2,1)} %pad_maximum_fusion.2), channel_id=1, source_target_pairs={{0,2},{1,3},{2,0},{3,1},{4,6},{5,7},{6,4},{7,5},{8,10},{9,11},{10,... | collective-permute-start | bytes 6291464 | tf_op jit(solution)/shard_map/ppermute | solution.py:17
  274.6 25.7 %copy-start.53 = (bf16[1024,1024]{1,0:T(8,128)(2,1)S(1)}, bf16[1024,1024]{1,0:T(8,128)(2,1)}, u32[]{:S(2)}) copy-start(bf16[1024,1024]{1,0:T(8,128)(2,1)} %param.35) | copy-start | bytes 6291460
  306.4 49.6 %copy-start.18 = (bf16[512,1024]{1,0:T(8,128)(2,1)S(1)}, bf16[512,1024]{1,0:T(8,128)(2,1)}, u32[]{:S(2)}) copy-start(bf16[512,1024]{1,0:T(8,128)(2,1)} %param.28) | copy-start | bytes 3145732
  306.4 199.8 %reduce-scatter.6.cloned.1.call-start = ((), (), s32[]{:S(2)}) async-start(), calls=%async_computation.4 | async-start | bytes 5242880 | tf_op jit(solution)/shard_map/reduce_scatter | solution.py:130
  360.6 12.4 %collective-permute-start.12 = (bf16[512,1024]{1,0:T(8,128)(2,1)S(1)}, bf16[512,1024]{1,0:T(8,128)(2,1)S(1)}, u32[]{:S(2)}, u32[]{:S(2)}) collective-permute-start(bf16[512,1024]{1,0:T(8,128)(2,1)S(1)} %get-tuple-element.32), channel_id=1, source_target_pairs={{0,3},{1,0},{2,1},{3,2},{4,7},{5,4},{6,5},{7,6},{8,11},{9,8},{10,9... | collective-permute-start | bytes 3145736 | tf_op jit(solution)/shard_map/ppermute | solution.py:17
  373.2 65.8 %copy-start.54 = (bf16[1024,1024]{1,0:T(8,128)(2,1)S(1)}, bf16[1024,1024]{1,0:T(8,128)(2,1)}, u32[]{:S(2)}) copy-start(bf16[1024,1024]{1,0:T(8,128)(2,1)} %param.35) | copy-start | bytes 6291460
  373.2 48.0 %collective-permute-start.13 = (bf16[1024,1024]{1,0:T(8,128)(2,1)S(1)}, bf16[1024,1024]{1,0:T(8,128)(2,1)S(1)}, u32[]{:S(2)}, u32[]{:S(2)}) collective-permute-start(bf16[1024,1024]{1,0:T(8,128)(2,1)S(1)} %pad_maximum_fusion.3), channel_id=1, source_target_pairs={{0,2},{1,3},{2,0},{3,1},{4,6},{5,7},{6,4},{7,5},{8,10},{9,11},{10,... | collective-permute-start | bytes 6291464 | tf_op jit(solution)/shard_map/ppermute | solution.py:17
  460.1 182.2 %reduce-scatter.8.cloned.1.call-start = ((), (), s32[]{:S(2)}) async-start(), calls=%async_computation.5 | async-start | bytes 10485760 | tf_op jit(solution)/shard_map/reduce_scatter | solution.py:130
  527.0 27.5 %copy-start.40 = (bf16[16,64,512]{2,1,0:T(8,128)(2,1)}, bf16[16,64,512]{2,1,0:T(8,128)(2,1)S(1)}, u32[]{:S(2)}) copy-start(bf16[16,64,512]{2,1,0:T(8,128)(2,1)S(1)} %get-tuple-element.73) | copy-start | bytes 3145732
  570.8 292.6 %all-reduce.3.cloned.1.call-start = ((), (), s32[]{:S(2)}) async-start(), calls=%async_computation.6 | async-start | bytes 12582912 | tf_op jit(solution)/shard_map/psum | solution.py:211
  (44 other events, 209.1 us)
Sparse Core Ops, SparseCore 0:
  306.5 46.4 reduce-scatter.3
  460.2 45.8 reduce-scatter.5
  570.9 71.3 reduce-scatter.7
  646.7 216.6 all-reduce.2
